TPU v7x, 512 devices: a whole 4x4x16 slice. The times are simulated.
512 devices in a mesh: row: 16 (over z_hi, y, core), col: 32 (over z_lo, x).
Axes of the slice: x: 4, y: 4, z: 16 (z_hi: 2, z_lo: 8; z = z_hi * 8 + z_lo), core: 2. Of those that a mesh axis runs over, the one named last changes fastest.
Arguments:
- amplitudes: bfloat16 [8192, 4096], P('row', 'col'), may hold values from -6 to 6
- packed_tiles: bfloat16 [16, 512, 128, 128], P('row', 'col'), may hold values from -0.09375 to 0.09375
- tile_ids: int32 [16, 512], P('row', 'col'), may hold values from 0 to 511, as said below
- residual_in: float32 [8192, 32768], P('row', 'col'), may hold values from -6 to 6
Outputs:
- ladder: float32 [8192, 32768], P('row', 'col')
Inputs may be any that keep to these rules, and one draw needn't show every extreme that they name: `tile_ids`: in each grid row the ids are a permutation of 0 to 511; no device holds more than 1 ids of one value of id // 16, and some device holds exactly 1.
All inputs are finite; a program needn't handle non-finite values.
Results may differ from a plain program's by a relative error of at most 0.0003.
Values may be sent and summed in bfloat16 or wider, within the bound.
A program may use at most 64 MiB of HBM per device.

v0:
```python
import jax
import jax.numpy as jnp
from jax import lax
from jax.sharding import PartitionSpec as P

KT_DEV = 2
QT_DEV = 8


def body(amplitudes, packed_tiles, tile_ids, residual_in):
    col_count = lax.axis_size("col")
    col_index = lax.axis_index("col")
    per_device = packed_tiles.shape[1]
    tile_width = packed_tiles.shape[2]
    capacity = (per_device + col_count - 1) // col_count
    slot_total = col_count * capacity
    own_ids = tile_ids[0]
    target_col = own_ids // per_device
    earlier = jnp.arange(per_device)[:, None] > jnp.arange(per_device)[None, :]
    same_target = target_col[:, None] == target_col[None, :]
    order_rank = jnp.sum(earlier & same_target, axis=1)
    slot_of = target_col * capacity + order_rank
    chooser = (jnp.arange(slot_total)[:, None] == slot_of[None, :]).astype(jnp.float32)
    outgoing = jnp.einsum(
        "sl,lij->sij",
        chooser.astype(jnp.bfloat16),
        packed_tiles[0],
        preferred_element_type=jnp.float32,
    )
    outgoing = outgoing.astype(jnp.bfloat16).reshape(col_count, capacity, tile_width, tile_width)
    all_ids = lax.all_gather(tile_ids, "col", axis=1, tiled=True)[0]
    incoming = lax.all_to_all(outgoing, "col", split_axis=0, concat_axis=0, tiled=True)
    source_ids = all_ids.reshape(col_count, per_device)
    source_target = source_ids // per_device
    source_same = source_target[:, :, None] == source_target[:, None, :]
    source_rank = jnp.sum(source_same & earlier[None], axis=2)
    source_slot = (jnp.arange(col_count)[:, None] * capacity + source_rank).reshape(-1)
    for_me = (source_target == col_index).reshape(-1)
    source_pos = (source_ids % per_device).reshape(-1)
    pos_table = ((jnp.arange(per_device)[:, None] == source_pos[None, :]) & for_me[None, :]).astype(
        jnp.float32
    )
    slot_table = (jnp.arange(slot_total)[:, None] == source_slot[None, :]).astype(jnp.float32)
    unpack = jnp.dot(pos_table, slot_table.T)
    unpacked = jnp.einsum(
        "ps,sij->pij",
        unpack.astype(jnp.bfloat16),
        incoming.reshape(slot_total, tile_width, tile_width),
        preferred_element_type=jnp.float32,
    )
    unpacked = unpacked.astype(jnp.bfloat16).reshape(KT_DEV, QT_DEV, tile_width, tile_width)
    integral_block = unpacked.transpose(0, 2, 1, 3).reshape(
        KT_DEV * tile_width, QT_DEV * tile_width
    )
    amp_full = lax.all_gather(amplitudes, "col", axis=1, tiled=True)
    product = jnp.dot(
        amp_full,
        lax.all_gather(integral_block, "row", axis=0, tiled=True),
        preferred_element_type=jnp.float32,
    )
    return residual_in + product


def solution(mesh):
    in_specs = (P("row", "col"), P("row", "col", None, None), P("row", "col"), P("row", "col"))
    out_specs = P("row", "col")
    return jax.shard_map(body, mesh=mesh, in_specs=in_specs, out_specs=out_specs, check_vma=False)
```

profile of v0, /device:TPU:1, one launch (start us, length us, event | category | flops | bytes accessed | tf_op | source)
XLA Modules:
  0.0 408.5 jit_solution(14928709801954503088)
XLA Ops:
  6.5 0.0 copy-start
  6.5 0.0 all-gather.5.cloned.1.call-start
  6.5 0.7 all-gather.5.cloned.1.call-update
  7.3 1.3 dynamic-slice
  9.2 0.7 fusion.23
  9.9 0.7 bitcast_dynamic-update-slice_fusion
  10.6 0.2 convert_reduce_fusion.1
  10.8 0.7 fusion.20
  11.5 0.0 copy-done
  11.5 0.6 fusion
  12.1 1.4 copy.22
  13.4 15.9 %all-to-all-start = ((bf16[32,1,128,128]{3,2,1,0:T(8,128)(2,1)}), bf16[32,1,128,128]{3,2,1,0:T(8,128)(2,1)S(1)}, u32[]{:S(2)}, u32[]{:S(2)}) async-start(bf16[32,1,128,128]{3,2,1,0:T(8,128)(2,1)} %copy.22), calls=%async_computation | async-start | bytes 2097152 | tf_op jit(solution)/shard_map/all_to_all | solution.py:32
  29.4 0.0 all-gather.3.cloned.1.call-start
  29.4 58.7 %all-reduce = s32[512]{0:T(512)S(1)} all-reduce(s32[512]{0:T(512)S(1)} %get-tuple-element.7), channel_id=1, replica_groups=mesh['row'=16,'col'=32] {'col'}, use_global_device_ids=true, to_apply=%add | all-reduce | flops 512 | bytes 4096
  88.2 0.1 reshape_squeeze.3
  88.3 0.1 copy.18
  88.3 0.1 convert_reduce_fusion
  88.5 0.1 copy.20
  88.5 0.1 add.51
  88.7 0.0 all-to-all-done
  88.7 0.7 fusion.1
  89.5 0.9 copy.35
  90.4 0.0 all-gather.3.cloned.1.call-update
  90.4 1.9 copy.25
  92.3 105.3 %all-gather.5.cloned.1.call-done = bf16[512,4096]{1,0:T(8,128)(2,1)} async-done(((bf16[512,128]{1,0:T(8,128)(2,1)}), bf16[512,4096]{1,0:T(8,128)(2,1)}) %all-gather.5.cloned.1.call-update) | async-done | bytes 4194320 | tf_op jit(solution)/shard_map/all_gather | solution.py:55
  197.6 190.7 %all-gather.3.cloned.1.call-done = bf16[4096,1024]{1,0:T(8,128)(2,1)} async-done(((bf16[256,1024]{1,0:T(8,128)(2,1)}), bf16[4096,1024]{1,0:T(8,128)(2,1)}) %all-gather.3.cloned.1.call-update) | async-done | bytes 8388624 | tf_op jit(solution)/shard_map/all_gather | solution.py:58
  388.3 10.5 %bitcast_add_fusion = f32[512,1024]{0,1:T(8,128)} fusion(f32[512,1024]{0,1:T(8,128)S(1)} %copy.25, bf16[4096,1024]{1,0:T(8,128)(2,1)} %all-gather.3.cloned.1.call-done, bf16[512,4096]{1,0:T(8,128)(2,1)} %all-gather.5.cloned.1.call-done), kind=kOutput, calls=%fused_computation | convolution fusion | flops 4295491584 | bytes 16777216 | tf_op jit(solution)/shard_map/dot_general | solution.py:56
  398.8 2.9 copy.26
  (7 shorter events, 0.1 us)
Async XLA Ops:
  6.5 4.9 %copy-start = (bf16[1,16,128,128]{3,2,1,0:T(8,128)(2,1)S(1)}, bf16[1,16,128,128]{3,2,1,0:T(8,128)(2,1)}, u32[]{:S(2)}) copy-start(bf16[1,16,128,128]{3,2,1,0:T(8,128)(2,1)} %param.5) | copy-start | bytes 1572868
  6.5 191.1 %all-gather.5.cloned.1.call-start = ((), (), s32[]{:S(2)}) async-start(), calls=%async_computation.2 | async-start | bytes 4325376 | tf_op jit(solution)/shard_map/all_gather | solution.py:55
  13.4 75.2 %all-to-all-start = ((bf16[32,1,128,128]{3,2,1,0:T(8,128)(2,1)}), bf16[32,1,128,128]{3,2,1,0:T(8,128)(2,1)S(1)}, u32[]{:S(2)}, u32[]{:S(2)}) async-start(bf16[32,1,128,128]{3,2,1,0:T(8,128)(2,1)} %copy.22), calls=%async_computation | async-start | bytes 2097152 | tf_op jit(solution)/shard_map/all_to_all | solution.py:32
  29.4 359.0 %all-gather.3.cloned.1.call-start = ((), (), s32[]{:S(2)}) async-start(), calls=%async_computation.1 | async-start | bytes 8912896 | tf_op jit(solution)/shard_map/all_gather | solution.py:58
Sparse Core Ops, SparseCore 0:
  9.4 188.2 all-gather.4
  200.9 187.3 all-gather.2
where the time goes:
time: 409 us
  waiting for transfers between devices  297 us (73%)
  blocking collectives  58.7 us (14%)
  starting transfers between devices  16 us (4%)
  between operations  14.1 us (3%)
  matrix products  11.8 us (3%)
  local copies, waits for them, and re-layouts  8.69 us (2%)
    all_gather x1, waiting for transfers between devices, body(): lax.all_gather(integral_block, 'row', axis=0, tiled=True)  191 us
    all_gather x1, waiting for transfers between devices, body(): amp_full = lax.all_gather(amplitudes, 'col', axis=1, tiled=True)  105 us
    unnamed x1, blocking collectives  58.7 us
    all_to_all x1, starting transfers between devices, body(): lax.all_to_all(outgoing, 'col', split_axis=0, concat_axis=0, tiled=True)  15.9 us
    dot_general x1, matrix products, body(): jnp.dot(amp_full, lax.all_gather(integral_block, 'row', axis=0, tiled=Tru...  10.5 us
  transfers between devices with their start and end apart: 3, of which 2 were waited for; matrix products, arithmetic and copies ran while one was open for 2% of the time, Pallas kernels for 0%

commit v1 on v0

--- a/solution.py
+++ b/solution.py
@@ -55,7 +55,9 @@
     amp_full = lax.all_gather(amplitudes, "col", axis=1, tiled=True)
     product = jnp.dot(
         amp_full,
-        lax.all_gather(integral_block, "row", axis=0, tiled=True),
+        jnp.concatenate(
+            lax.all_to_all(jnp.stack([integral_block] * lax.axis_size("row")), "row", 0, 0), axis=0
+        ),
         preferred_element_type=jnp.float32,
     )
     return residual_in + product

time: 409 us -> 631 us (1.54); the launches traced: 409 us -> 623 us
  waiting for transfers between devices: 297 us -> 506 us
  starting transfers between devices: 16 us -> 28.9 us
  blocking collectives: 58.7 us -> 50 us
    all_gather x1, waiting for transfers between devices: 105 us -> 505 us  [body(): amp_full = lax.all_gather(amplitudes, 'col', axis=1, tiled=True)]
    all_gather x1 -> x0, waiting for transfers between devices: 191 us -> none  [body(): lax.all_gather(integral_block, 'row', axis=0, tiled=True)]
    all_to_all x0 -> x1, starting transfers between devices: none -> 12.9 us  [body(): lax.all_to_all(jnp.stack([integral_block] * lax.axis_size('row')), 'row',...]
    unnamed x1, blocking collectives: 58.7 us -> 50 us
  transfers between devices with their start and end apart: 3 -> 3, of which waited for: 2 -> 1; matrix products, arithmetic and copies ran while one was open for 2% -> 0% of each run, Pallas kernels for 0% -> 0%
where the time goes in v1:
time: 631 us; the launch traced here: 623 us
  waiting for transfers between devices  506 us (80%)
  blocking collectives  50 us (8%)
  starting transfers between devices  28.9 us (5%)
  between operations  14.2 us (2%)
  matrix products  11.1 us (2%)
  local copies, waits for them, and re-layouts  11 us (2%)
    all_gather x1, waiting for transfers between devices, body(): amp_full = lax.all_gather(amplitudes, 'col', axis=1, tiled=True)  505 us
    unnamed x1, blocking collectives  50 us
    all_to_all x1, starting transfers between devices, body(): lax.all_to_all(outgoing, 'col', split_axis=0, concat_axis=0, tiled=True)  15.9 us
    all_to_all x1, starting transfers between devices, body(): lax.all_to_all(jnp.stack([integral_block] * lax.axis_size('row')), 'row',...  12.9 us
  transfers between devices with their start and end apart: 3, of which 1 were waited for; matrix products, arithmetic and copies ran while one was open for 0% of the time, Pallas kernels for 0%

profile of v1, /device:TPU:1, one launch (start us, length us, event | category | flops | bytes accessed | tf_op | source)
XLA Modules:
  0.0 623.3 jit_solution(13609303106781571814)
XLA Ops:
  6.5 0.0 copy-start
  6.5 0.7 fusion.23
  7.3 1.3 dynamic-slice
  9.2 0.8 bitcast_dynamic-update-slice_fusion
  9.9 0.2 convert_reduce_fusion.1
  10.1 0.7 fusion.20
  10.8 0.0 copy-done
  10.8 0.6 fusion
  11.4 1.4 copy.22
  12.8 15.9 %all-to-all-start = ((bf16[32,1,128,128]{3,2,1,0:T(8,128)(2,1)}), bf16[32,1,128,128]{3,2,1,0:T(8,128)(2,1)S(1)}, u32[]{:S(2)}, u32[]{:S(2)}) async-start(bf16[32,1,128,128]{3,2,1,0:T(8,128)(2,1)} %copy.22), calls=%async_computation | async-start | bytes 2097152 | tf_op jit(solution)/shard_map/all_to_all | solution.py:32
  28.7 50.0 %all-reduce = s32[512]{0:T(512)S(1)} all-reduce(s32[512]{0:T(512)S(1)} %get-tuple-element.7), channel_id=1, replica_groups=mesh['row'=16,'col'=32] {'col'}, use_global_device_ids=true, to_apply=%add | all-reduce | flops 512 | bytes 4096
  78.7 0.1 reshape_squeeze.3
  78.8 0.1 copy.18
  78.9 0.1 convert_reduce_fusion
  79.0 0.1 copy.20
  79.1 0.1 add.51
  79.2 0.0 all-to-all-done
  79.2 0.7 fusion.1
  80.0 0.1 copy.35
  80.1 4.3 stack.3
  84.4 0.0 copy-start.1
  84.4 12.9 %all-to-all-start.1 = ((bf16[16,256,1024]{2,1,0:T(8,128)(2,1)}), bf16[16,256,1024]{2,1,0:T(8,128)(2,1)}, u32[]{:S(2)}, u32[]{:S(2)}) async-start(bf16[16,256,1024]{2,1,0:T(8,128)(2,1)} %stack.3), calls=%async_computation.1 | async-start | bytes 16777216 | tf_op jit(solution)/shard_map/all_to_all | solution.py:59
  97.3 0.0 all-gather.2.cloned.1.call-start
  97.4 0.7 all-gather.2.cloned.1.call-update
  98.1 0.0 copy-done.1
  98.1 1.8 copy.25
  99.9 504.9 %all-gather.2.cloned.1.call-done = bf16[512,4096]{1,0:T(8,128)(2,1)} async-done(((bf16[512,128]{1,0:T(8,128)(2,1)}), bf16[512,4096]{1,0:T(8,128)(2,1)}) %all-gather.2.cloned.1.call-update) | async-done | bytes 4194320 | tf_op jit(solution)/shard_map/all_gather | solution.py:55
  604.8 0.0 all-to-all-done.1
  604.8 9.8 %bitcast_add_fusion = f32[512,1024]{0,1:T(8,128)S(1)} fusion(f32[512,1024]{0,1:T(8,128)} %copy.25, bf16[4096,1024]{1,0:T(8,128)(2,1)} %bitcast.14, bf16[512,4096]{1,0:T(8,128)(2,1)} %all-gather.2.cloned.1.call-done), kind=kOutput, calls=%fused_computation | convolution fusion | flops 4295491584 | bytes 16777216 | tf_op jit(solution)/shard_map/dot_general | solution.py:56
  614.6 1.8 copy.26
  (7 shorter events, 0.1 us)
Async XLA Ops:
  6.5 4.3 copy-start
  12.8 66.4 %all-to-all-start = ((bf16[32,1,128,128]{3,2,1,0:T(8,128)(2,1)}), bf16[32,1,128,128]{3,2,1,0:T(8,128)(2,1)S(1)}, u32[]{:S(2)}, u32[]{:S(2)}) async-start(bf16[32,1,128,128]{3,2,1,0:T(8,128)(2,1)} %copy.22), calls=%async_computation | async-start | bytes 2097152 | tf_op jit(solution)/shard_map/all_to_all | solution.py:32
  84.4 13.7 %copy-start.1 = (f32[512,1024]{1,0:T(8,128)S(1)}, f32[512,1024]{1,0:T(8,128)}, u32[]{:S(2)}) copy-start(f32[512,1024]{1,0:T(8,128)} %param.7) | copy-start | bytes 6291460
  84.4 520.4 %all-to-all-start.1 = ((bf16[16,256,1024]{2,1,0:T(8,128)(2,1)}), bf16[16,256,1024]{2,1,0:T(8,128)(2,1)}, u32[]{:S(2)}, u32[]{:S(2)}) async-start(bf16[16,256,1024]{2,1,0:T(8,128)(2,1)} %stack.3), calls=%async_computation.1 | async-start | bytes 16777216 | tf_op jit(solution)/shard_map/all_to_all | solution.py:59
  97.3 507.5 %all-gather.2.cloned.1.call-start = ((), (), s32[]{:S(2)}) async-start(), calls=%async_computation.2 | async-start | bytes 4325376 | tf_op jit(solution)/shard_map/all_gather | solution.py:55
Sparse Core Ops, SparseCore 0:
  100.2 504.5 all-gather.1
